TPU v7x, 32 devices: a whole 2x2x4 slice. The times are simulated.
32 devices in a mesh: vec: 4 (over x, core), lat: 8 (over z, y).
Axes of the slice: x: 2, y: 2, z: 4, core: 2. Of those that a mesh axis runs over, the one named last changes fastest.
Arguments:
- perturbation: float32 [32, 3, 64, 2048], P('vec', None, 'lat'), may hold values from -6 to 6
- wind_coriolis: float32 [4, 3, 64, 2048], P(None, None, 'lat', 'vec'), may hold values from -4 to 4
- depth_field: float32 [4, 64, 2048], P(None, 'lat', 'vec'), may hold values from 0.5 to 2
Outputs:
- evolved: float32 [32, 3, 64, 2048], P('vec', None, 'lat')
All inputs are finite; a program needn't handle non-finite values.
Results may differ from a plain program's by a relative error of at most 0.00002.
Values sent between devices are 32-bit elements; how exact they have to be, the bound alone decides.
A program may use at most 64 MiB of HBM per device.

v0:
```python
import jax
import jax.numpy as jnp
from jax import lax
from jax.sharding import PartitionSpec as P

STEPS = 4


time_step = 0.2
viscosity = 0.05


def extended(shard, sides, width):
    for axis, dim in sides:
        count, length = (lax.axis_size(axis), shard.shape[dim])
        up = [(i, (i + 1) % count) for i in range(count - 1)]
        down = [(j, i) for i, j in up]
        last = lax.slice_in_dim(shard, length - width, length, axis=dim)
        leading = lax.slice_in_dim(shard, 0, width, axis=dim)
        before = lax.ppermute(last, axis, up)
        after = lax.ppermute(leading, axis, down)
        shard = jnp.concatenate([before, shard, after], axis=dim)
    return shard


def lon_diff(field):
    return 0.5 * (jnp.roll(field, -1, axis=-1) - jnp.roll(field, 1, axis=-1))


def lat_diff(padded):
    return 0.5 * (padded[..., 2:, :] - padded[..., :-2, :])


def smooth(padded, centre):
    return (
        padded[..., 2:, :]
        + padded[..., :-2, :]
        + jnp.roll(centre, -1, axis=-1)
        + jnp.roll(centre, 1, axis=-1)
        - 4.0 * centre
    )


def advance(padded, coefficients):
    height_pad = padded[..., 0, :, :]
    zonal_pad = padded[..., 1, :, :]
    north_pad = padded[..., 2, :, :]
    height = height_pad[..., 1:-1, :]
    zonal = zonal_pad[..., 1:-1, :]
    north = north_pad[..., 1:-1, :]
    east_wind = coefficients[0]
    north_wind = coefficients[1]
    rotation = coefficients[2]
    depth_now = coefficients[3]
    tend_height = -(
        east_wind * lon_diff(height)
        + north_wind * lat_diff(height_pad)
        + depth_now * (lon_diff(zonal) + lat_diff(north_pad))
    )
    tend_zonal = (
        -(east_wind * lon_diff(zonal) + north_wind * lat_diff(zonal_pad))
        + rotation * north
        - lon_diff(height)
    )
    tend_north = (
        -(east_wind * lon_diff(north) + north_wind * lat_diff(north_pad))
        - rotation * zonal
        - lat_diff(height_pad)
    )
    new_height = height + time_step * (tend_height + viscosity * smooth(height_pad, height))
    new_zonal = zonal + time_step * (tend_zonal + viscosity * smooth(zonal_pad, zonal))
    new_north = north + time_step * (tend_north + viscosity * smooth(north_pad, north))
    return jnp.stack([new_height, new_zonal, new_north], axis=-3)


def shards(perturbation, wind_coriolis, depth_field):
    coefficients = jnp.concatenate([wind_coriolis, depth_field[:, None]], axis=1)
    state = perturbation
    for moment in range(STEPS):
        gathered = lax.all_gather(coefficients[moment], "vec", axis=2, tiled=True)
        padded = extended(state, (("lat", 2),), 1)
        state = advance(padded, gathered)
    return state


def solution(mesh):
    placed = (P("vec", None, "lat", None), P(None, None, "lat", "vec"), P(None, "lat", "vec"))
    return jax.shard_map(
        shards, mesh=mesh, in_specs=placed, out_specs=P("vec", None, "lat", None), check_vma=False
    )
```

profile of v0, /device:TPU:9, one launch (start us, length us, event | category | flops | bytes accessed | tf_op | source)
XLA Modules:
  0.0 80.3 jit_solution(6059171773008003031)
XLA Ops:
  0.0 2.3 %fusion.23 = (f32[8,3,1,2048]{3,2,0,1:T(1,128)S(1)}, f32[8,3,1,2048]{3,2,0,1:T(1,128)S(1)}) fusion(f32[8,3,8,2048]{3,2,1,0:T(8,128)} %param.3), kind=kLoop, calls=%fused_computation.116 | loop fusion | bytes 786432 | tf_op jit(solution)/shard_map/slice | solution.py:18
  2.4 3.1 %collective-permute-start = (f32[8,3,1,2048]{3,2,0,1:T(1,128)S(1)}, f32[8,3,1,2048]{3,2,0,1:T(1,128)S(1)}, u32[]{:S(2)}, u32[]{:S(2)}) collective-permute-start(f32[8,3,1,2048]{3,2,0,1:T(1,128)S(1)} %get-tuple-element.23), channel_id=1, source_target_pairs={{0,1},{1,2},{2,3},{3,4},{4,5},{5,6},{6,7},{8,9},{9,10},{10,11},{11... | collective-permute-start | bytes 589832 | tf_op jit(solution)/shard_map/ppermute | solution.py:20
  5.5 3.0 %collective-permute-start.1 = (f32[8,3,1,2048]{3,2,0,1:T(1,128)S(1)}, f32[8,3,1,2048]{3,2,0,1:T(1,128)S(1)}, u32[]{:S(2)}, u32[]{:S(2)}) collective-permute-start(f32[8,3,1,2048]{3,2,0,1:T(1,128)S(1)} %get-tuple-element.24), channel_id=1, source_target_pairs={{1,0},{2,1},{3,2},{4,3},{5,4},{6,5},{7,6},{9,8},{10,9},{11,10},{12... | collective-permute-start | bytes 589832 | tf_op jit(solution)/shard_map/ppermute | solution.py:21
  8.6 1.0 %pad_maximum_fusion.38 = (f32[1,4,8,512]{3,2,1,0:T(8,128)S(1)}, f32[1,4,8,512]{3,2,1,0:T(8,128)S(1)}, f32[1,4,8,512]{3,2,1,0:T(8,128)S(1)}, f32[1,4,8,512]{3,2,1,0:T(8,128)S(1)}) fusion(f32[4,1,8,512]{3,2,1,0:T(8,128)} %bitcast.87, f32[4,3,8,512]{3,2,1,0:T(8,128)} %param.4), kind=kLoop, calls=%fused_computation.94 | loop fusion | flops 65536 | bytes 524288 | tf_op jit(solution)/shard_map/concatenate | solution.py:77
  9.5 6.8 %all-gather = f32[1,4,8,2048]{3,2,1,0:T(8,128)S(1)} all-gather(f32[1,4,8,512]{3,2,1,0:T(8,128)S(1)} %get-tuple-element.78), channel_id=2, replica_groups=mesh['vec'=4,'lat'=8] {'vec'}, dimensions={3}, use_global_device_ids=true | all-gather | bytes 327680 | tf_op jit(solution)/shard_map/all_gather | solution.py:80
  16.4 5.9 %all-gather.1 = f32[1,4,8,2048]{3,2,1,0:T(8,128)S(1)} all-gather(f32[1,4,8,512]{3,2,1,0:T(8,128)S(1)} %get-tuple-element.79), channel_id=3, replica_groups=mesh['vec'=4,'lat'=8] {'vec'}, dimensions={3}, use_global_device_ids=true | all-gather | bytes 327680 | tf_op jit(solution)/shard_map/all_gather | solution.py:80
  23.9 0.6 add_bitcast_fusion.11
  24.6 0.6 add_bitcast_fusion.10
  25.2 0.6 add_bitcast_fusion.9
  26.0 2.2 %collective-permute-start.2 = (f32[8,3,1,2048]{3,2,0,1:T(1,128)S(1)}, f32[8,3,1,2048]{3,2,0,1:T(1,128)S(1)}, u32[]{:S(2)}, u32[]{:S(2)}) collective-permute-start(f32[8,3,1,2048]{3,2,0,1:T(1,128)S(1)} %get-tuple-element.21), channel_id=1, source_target_pairs={{0,1},{1,2},{2,3},{3,4},{4,5},{5,6},{6,7},{8,9},{9,10},{10,11},{11... | collective-permute-start | bytes 589832 | tf_op jit(solution)/shard_map/ppermute | solution.py:20
  28.3 3.9 %collective-permute-start.3 = (f32[8,3,1,2048]{3,2,0,1:T(1,128)S(1)}, f32[8,3,1,2048]{3,2,0,1:T(1,128)S(1)}, u32[]{:S(2)}, u32[]{:S(2)}) collective-permute-start(f32[8,3,1,2048]{3,2,0,1:T(1,128)S(1)} %get-tuple-element.22), channel_id=1, source_target_pairs={{1,0},{2,1},{3,2},{4,3},{5,4},{6,5},{7,6},{9,8},{10,9},{11,10},{12... | collective-permute-start | bytes 589832 | tf_op jit(solution)/shard_map/ppermute | solution.py:21
  32.3 6.3 %all-gather.2 = f32[1,4,8,2048]{3,2,1,0:T(8,128)S(1)} all-gather(f32[1,4,8,512]{3,2,1,0:T(8,128)S(1)} %get-tuple-element.80), channel_id=4, replica_groups=mesh['vec'=4,'lat'=8] {'vec'}, dimensions={3}, use_global_device_ids=true | all-gather | bytes 327680 | tf_op jit(solution)/shard_map/all_gather | solution.py:80
  38.6 1.3 %collective-permute-done.3 = f32[8,3,1,2048]{3,2,0,1:T(1,128)S(1)} collective-permute-done((f32[8,3,1,2048]{3,2,0,1:T(1,128)S(1)}, f32[8,3,1,2048]{3,2,0,1:T(1,128)S(1)}, u32[]{:S(2)}, u32[]{:S(2)}) %collective-permute-start.3) | collective-permute-done | bytes 196640 | tf_op jit(solution)/shard_map/ppermute | solution.py:21
  39.9 0.6 pad_maximum_fusion.1
  41.7 0.6 add_bitcast_fusion.8
  42.3 0.6 add_bitcast_fusion.7
  43.0 0.6 add_bitcast_fusion.6
  43.8 1.9 %collective-permute-start.4 = (f32[8,3,1,2048]{3,2,0,1:T(1,128)S(1)}, f32[8,3,1,2048]{3,2,0,1:T(1,128)S(1)}, u32[]{:S(2)}, u32[]{:S(2)}) collective-permute-start(f32[8,3,1,2048]{3,2,0,1:T(1,128)S(1)} %get-tuple-element.19), channel_id=1, source_target_pairs={{0,1},{1,2},{2,3},{3,4},{4,5},{5,6},{6,7},{8,9},{9,10},{10,11},{11... | collective-permute-start | bytes 589832 | tf_op jit(solution)/shard_map/ppermute | solution.py:20
  45.8 4.3 %collective-permute-start.5 = (f32[8,3,1,2048]{3,2,0,1:T(1,128)S(1)}, f32[8,3,1,2048]{3,2,0,1:T(1,128)S(1)}, u32[]{:S(2)}, u32[]{:S(2)}) collective-permute-start(f32[8,3,1,2048]{3,2,0,1:T(1,128)S(1)} %get-tuple-element.20), channel_id=1, source_target_pairs={{1,0},{2,1},{3,2},{4,3},{5,4},{6,5},{7,6},{9,8},{10,9},{11,10},{12... | collective-permute-start | bytes 589832 | tf_op jit(solution)/shard_map/ppermute | solution.py:21
  50.0 6.8 %all-gather.3 = f32[1,4,8,2048]{3,2,1,0:T(8,128)S(1)} all-gather(f32[1,4,8,512]{3,2,1,0:T(8,128)S(1)} %get-tuple-element.77), channel_id=5, replica_groups=mesh['vec'=4,'lat'=8] {'vec'}, dimensions={3}, use_global_device_ids=true | all-gather | bytes 327680 | tf_op jit(solution)/shard_map/all_gather | solution.py:80
  56.9 0.8 collective-permute-done.5
  59.5 0.6 add_bitcast_fusion.5
  60.1 0.6 add_bitcast_fusion.4
  60.7 0.6 add_bitcast_fusion.3
  61.6 1.9 %collective-permute-start.6 = (f32[8,3,1,2048]{3,2,0,1:T(1,128)S(1)}, f32[8,3,1,2048]{3,2,0,1:T(1,128)S(1)}, u32[]{:S(2)}, u32[]{:S(2)}) collective-permute-start(f32[8,3,1,2048]{3,2,0,1:T(1,128)S(1)} %get-tuple-element.17), channel_id=1, source_target_pairs={{0,1},{1,2},{2,3},{3,4},{4,5},{5,6},{6,7},{8,9},{9,10},{10,11},{11... | collective-permute-start | bytes 589832 | tf_op jit(solution)/shard_map/ppermute | solution.py:20
  63.5 4.3 %collective-permute-start.7 = (f32[8,3,1,2048]{3,2,0,1:T(1,128)S(1)}, f32[8,3,1,2048]{3,2,0,1:T(1,128)S(1)}, u32[]{:S(2)}, u32[]{:S(2)}) collective-permute-start(f32[8,3,1,2048]{3,2,0,1:T(1,128)S(1)} %get-tuple-element.18), channel_id=1, source_target_pairs={{1,0},{2,1},{3,2},{4,3},{5,4},{6,5},{7,6},{9,8},{10,9},{11,10},{12... | collective-permute-start | bytes 589832 | tf_op jit(solution)/shard_map/ppermute | solution.py:21
  67.8 2.5 %collective-permute-done.6 = f32[8,3,1,2048]{3,2,0,1:T(1,128)S(1)} collective-permute-done((f32[8,3,1,2048]{3,2,0,1:T(1,128)S(1)}, f32[8,3,1,2048]{3,2,0,1:T(1,128)S(1)}, u32[]{:S(2)}, u32[]{:S(2)}) %collective-permute-start.6) | collective-permute-done | bytes 196640 | tf_op jit(solution)/shard_map/ppermute | solution.py:20
  70.3 5.1 %collective-permute-done.7 = f32[8,3,1,2048]{3,2,0,1:T(1,128)S(1)} collective-permute-done((f32[8,3,1,2048]{3,2,0,1:T(1,128)S(1)}, f32[8,3,1,2048]{3,2,0,1:T(1,128)S(1)}, u32[]{:S(2)}, u32[]{:S(2)}) %collective-permute-start.7) | collective-permute-done | bytes 196640 | tf_op jit(solution)/shard_map/ppermute | solution.py:21
  77.2 0.6 add_bitcast_fusion.2
  77.8 0.6 add_bitcast_fusion.1
  78.4 0.6 add_bitcast_fusion
  79.0 1.3 %pad_maximum_fusion.4 = f32[8,3,8,2048]{3,2,1,0:T(8,128)} fusion(f32[8,1,8,2048]{3,2,1,0:T(8,128)S(1)} %add_bitcast_fusion, f32[8,1,8,2048]{3,2,1,0:T(8,128)S(1)} %add_bitcast_fusion.1, f32[8,1,8,2048]{3,2,1,0:T(8,128)S(1)} %add_bitcast_fusion.2), kind=kLoop, calls=%fused_computation.4 | loop fusion | flops 786432 | bytes 3145728 | tf_op jit(solution)/shard_map/stack | solution.py:73
  (42 shorter events, 7.3 us)
Async XLA Ops:
  0.0 22.2 %copy-start = (f32[8,3,8,2048]{3,2,1,0:T(8,128)S(1)}, f32[8,3,8,2048]{3,2,1,0:T(8,128)}, u32[]{:S(2)}) copy-start(f32[8,3,8,2048]{3,2,1,0:T(8,128)} %param.3) | copy-start | bytes 4718596
  2.4 19.9 %collective-permute-start = (f32[8,3,1,2048]{3,2,0,1:T(1,128)S(1)}, f32[8,3,1,2048]{3,2,0,1:T(1,128)S(1)}, u32[]{:S(2)}, u32[]{:S(2)}) collective-permute-start(f32[8,3,1,2048]{3,2,0,1:T(1,128)S(1)} %get-tuple-element.23), channel_id=1, source_target_pairs={{0,1},{1,2},{2,3},{3,4},{4,5},{5,6},{6,7},{8,9},{9,10},{10,11},{11... | collective-permute-start | bytes 589832 | tf_op jit(solution)/shard_map/ppermute | solution.py:20
  5.5 16.7 %collective-permute-start.1 = (f32[8,3,1,2048]{3,2,0,1:T(1,128)S(1)}, f32[8,3,1,2048]{3,2,0,1:T(1,128)S(1)}, u32[]{:S(2)}, u32[]{:S(2)}) collective-permute-start(f32[8,3,1,2048]{3,2,0,1:T(1,128)S(1)} %get-tuple-element.24), channel_id=1, source_target_pairs={{1,0},{2,1},{3,2},{4,3},{5,4},{6,5},{7,6},{9,8},{10,9},{11,10},{12... | collective-permute-start | bytes 589832 | tf_op jit(solution)/shard_map/ppermute | solution.py:21
  26.0 12.6 %collective-permute-start.2 = (f32[8,3,1,2048]{3,2,0,1:T(1,128)S(1)}, f32[8,3,1,2048]{3,2,0,1:T(1,128)S(1)}, u32[]{:S(2)}, u32[]{:S(2)}) collective-permute-start(f32[8,3,1,2048]{3,2,0,1:T(1,128)S(1)} %get-tuple-element.21), channel_id=1, source_target_pairs={{0,1},{1,2},{2,3},{3,4},{4,5},{5,6},{6,7},{8,9},{9,10},{10,11},{11... | collective-permute-start | bytes 589832 | tf_op jit(solution)/shard_map/ppermute | solution.py:20
  28.3 11.6 %collective-permute-start.3 = (f32[8,3,1,2048]{3,2,0,1:T(1,128)S(1)}, f32[8,3,1,2048]{3,2,0,1:T(1,128)S(1)}, u32[]{:S(2)}, u32[]{:S(2)}) collective-permute-start(f32[8,3,1,2048]{3,2,0,1:T(1,128)S(1)} %get-tuple-element.22), channel_id=1, source_target_pairs={{1,0},{2,1},{3,2},{4,3},{5,4},{6,5},{7,6},{9,8},{10,9},{11,10},{12... | collective-permute-start | bytes 589832 | tf_op jit(solution)/shard_map/ppermute | solution.py:21
  43.8 13.0 %collective-permute-start.4 = (f32[8,3,1,2048]{3,2,0,1:T(1,128)S(1)}, f32[8,3,1,2048]{3,2,0,1:T(1,128)S(1)}, u32[]{:S(2)}, u32[]{:S(2)}) collective-permute-start(f32[8,3,1,2048]{3,2,0,1:T(1,128)S(1)} %get-tuple-element.19), channel_id=1, source_target_pairs={{0,1},{1,2},{2,3},{3,4},{4,5},{5,6},{6,7},{8,9},{9,10},{10,11},{11... | collective-permute-start | bytes 589832 | tf_op jit(solution)/shard_map/ppermute | solution.py:20
  45.8 11.9 %collective-permute-start.5 = (f32[8,3,1,2048]{3,2,0,1:T(1,128)S(1)}, f32[8,3,1,2048]{3,2,0,1:T(1,128)S(1)}, u32[]{:S(2)}, u32[]{:S(2)}) collective-permute-start(f32[8,3,1,2048]{3,2,0,1:T(1,128)S(1)} %get-tuple-element.20), channel_id=1, source_target_pairs={{1,0},{2,1},{3,2},{4,3},{5,4},{6,5},{7,6},{9,8},{10,9},{11,10},{12... | collective-permute-start | bytes 589832 | tf_op jit(solution)/shard_map/ppermute | solution.py:21
  61.6 8.8 %collective-permute-start.6 = (f32[8,3,1,2048]{3,2,0,1:T(1,128)S(1)}, f32[8,3,1,2048]{3,2,0,1:T(1,128)S(1)}, u32[]{:S(2)}, u32[]{:S(2)}) collective-permute-start(f32[8,3,1,2048]{3,2,0,1:T(1,128)S(1)} %get-tuple-element.17), channel_id=1, source_target_pairs={{0,1},{1,2},{2,3},{3,4},{4,5},{5,6},{6,7},{8,9},{9,10},{10,11},{11... | collective-permute-start | bytes 589832 | tf_op jit(solution)/shard_map/ppermute | solution.py:20
  63.5 11.9 %collective-permute-start.7 = (f32[8,3,1,2048]{3,2,0,1:T(1,128)S(1)}, f32[8,3,1,2048]{3,2,0,1:T(1,128)S(1)}, u32[]{:S(2)}, u32[]{:S(2)}) collective-permute-start(f32[8,3,1,2048]{3,2,0,1:T(1,128)S(1)} %get-tuple-element.18), channel_id=1, source_target_pairs={{1,0},{2,1},{3,2},{4,3},{5,4},{6,5},{7,6},{9,8},{10,9},{11,10},{12... | collective-permute-start | bytes 589832 | tf_op jit(solution)/shard_map/ppermute | solution.py:21
where the time goes:
time: 80.7 us; the launch traced here: 80.3 us
  blocking collectives  25.9 us (32%)
  starting transfers between devices  24.7 us (31%)
  other arithmetic  12.6 us (16%)
  waiting for transfers between devices  9.72 us (12%)
  local copies, waits for them, and re-layouts  7.08 us (9%)
    all_gather x4, blocking collectives, shards(): gathered = lax.all_gather(coefficients[moment], 'vec', axis=2, tiled=True)  25.9 us
    ppermute x4, starting transfers between devices, extended(): after = lax.ppermute(leading, axis, down)  15.5 us
    ppermute x4, starting transfers between devices, extended(): before = lax.ppermute(last, axis, up)  9.24 us
    another operation x13, other arithmetic, advance(): return jnp.stack([new_height, new_zonal, new_north], axis=-3)  8.52 us
    ppermute x4, waiting for transfers between devices, extended(): after = lax.ppermute(leading, axis, down)  7.17 us
    slice x22, local copies, waits for them, and re-layouts, lon_diff(): return 0.5 * (jnp.roll(field, -1, axis=-1) - jnp.roll(field, 1, axis=-1))  3.37 us
    ppermute x4, waiting for transfers between devices, extended(): before = lax.ppermute(last, axis, up)  2.55 us
    slice x1, local copies, waits for them, and re-layouts, extended(): last = lax.slice_in_dim(shard, length - width, length, axis=dim)  2.34 us
  transfers between devices with their start and end apart: 8, of which 4 were waited for; matrix products, arithmetic and copies ran while one was open for 1% of the time, Pallas kernels for 0%

commit v1 on v0

v1 whole, which is shorter than its diff:
```python
import functools

import jax
import jax.numpy as jnp
from jax import lax
from jax.experimental import pallas as pl
from jax.experimental.pallas import tpu as pltpu
from jax.sharding import PartitionSpec as P

MESH = pl.DeviceIdType.MESH
LANES = 128
time_step = 0.2
viscosity = 0.05
side_weight = time_step * viscosity
half_step = 0.5 * time_step


def sweep(load, store, coefficient, sides, tiles, keep):
    lane = lax.broadcasted_iota(jnp.int32, (8, LANES), 1)
    row = lax.broadcasted_iota(jnp.int32, (8, LANES), 0)
    first_lane, last_lane = lane == 0, lane == LANES - 1
    first_row, last_row = row == 0, row == 7
    known = {}

    def tile(side, field, t):
        key = (side, field, t)
        if key not in known:
            value = load(side, field, t % tiles)
            known[key] = (value, pltpu.roll(value, LANES - 1, 1), pltpu.roll(value, 1, 1))
        return known[key]

    for t in range(tiles):
        east, west, rise, fall, here = {}, {}, {}, {}, {}
        for field in range(3):
            turned = []
            for side in range(2):
                value = tile(side, field, t)[0] if side in sides else load(side, field, t)
                turned.append((pltpu.roll(value, 7, 0), pltpu.roll(value, 1, 0)))
            for side in sides:
                before, now, after = (tile(side, field, t + k) for k in (-1, 0, 1))
                here[side, field] = now[0]
                east[side, field] = jnp.where(last_lane, after[1], now[1])
                west[side, field] = jnp.where(first_lane, before[2], now[2])
                rise[side, field] = jnp.where(last_row, turned[1 - side][0], turned[side][0])
                fall[side, field] = jnp.where(first_row, turned[1 - side][1], turned[side][1])
        for side in sides:
            a = half_step * coefficient(side, 0, t)
            b = half_step * coefficient(side, 1, t)
            d = time_step * coefficient(side, 2, t)
            c = half_step * coefficient(side, 3, t)
            to_east, to_west = side_weight - a, side_weight + a
            to_rise, to_fall = side_weight - b, side_weight + b
            new = [
                (1.0 - 4.0 * side_weight) * here[side, f]
                + (to_east * east[side, f] + to_west * west[side, f])
                + (to_rise * rise[side, f] + to_fall * fall[side, f])
                for f in range(3)
            ]
            new[0] -= c * ((east[side, 1] - west[side, 1]) + (rise[side, 2] - fall[side, 2]))
            new[1] += d * here[side, 2] - half_step * (east[side, 0] - west[side, 0])
            new[2] -= d * here[side, 1] + half_step * (rise[side, 0] - fall[side, 0])
            for f in range(3):
                store(side, f, t, new[f] if side == 0 else jnp.where(keep, new[f], 0.0))


def kernel(
    nv, nl, x_hbm, wind, depth, out_hbm,
    x, halo, ping, pong, out, own, ring,
    x_sem, own_sem, out_sem,
    gs, gr, cs, cr, fs, fr, hs, hr,
):
    count, _, rows, width = x_hbm.shape
    steps, part = wind.shape[0], wind.shape[3]
    tiles, reach = width // LANES, steps
    v, l = lax.axis_index("vec"), lax.axis_index("lat")
    has = (l > 0, l < nl - 1)
    other = (l - 1, l + 1)
    peers = [lax.rem(v + k, nv) for k in range(1, nv)]
    edge = (lambda n: pl.ds(0, n), lambda n: pl.ds(rows - n, n))

    local = [
        pltpu.make_async_copy(x_hbm, x, x_sem.at[0]),
        pltpu.make_async_copy(wind, own.at[v, :, pl.ds(0, 3)], own_sem.at[0]),
        pltpu.make_async_copy(depth, own.at[v, :, 3], own_sem.at[1]),
    ]
    for copy in local:
        copy.start()

    for side in range(2):
        @pl.when(jnp.logical_not(has[1 - side]))
        def _(side=side):
            halo[:, :, edge[side](reach), :] = jnp.zeros((count, 3, reach, width), jnp.float32)

    barrier = pltpu.get_barrier_semaphore()
    for peer in peers:
        pl.semaphore_signal(barrier, inc=1, device_id={"vec": peer}, device_id_type=MESH)
    for side in range(2):
        @pl.when(has[side])
        def _(side=side):
            pl.semaphore_signal(barrier, inc=1, device_id={"lat": other[side]}, device_id_type=MESH)
    pl.semaphore_wait(barrier, nv - 1 + has[0].astype(jnp.int32) + has[1].astype(jnp.int32))

    def remote(src, dst, send, recv, target):
        return pltpu.make_async_remote_copy(
            src_ref=src, dst_ref=dst, send_sem=send, recv_sem=recv,
            device_id=target, device_id_type=MESH,
        )

    def edges(side):
        made = []
        for s in range(steps - 1):
            at = edge[side](reach - 1 - s)
            made.append(remote(
                wind.at[s, :, at, :], ring.at[v, s, pl.ds(0, 3), at, :],
                cs.at[side, s, 0], cr.at[side, s, 0], {"lat": other[side]}))
            made.append(remote(
                depth.at[s, at, :], ring.at[v, s, 3, at, :],
                cs.at[side, s, 1], cr.at[side, s, 1], {"lat": other[side]}))
        return made

    def state(side, k):
        at = edge[side](reach)
        return remote(
            x_hbm.at[k, :, at, :], halo.at[k, :, at, :],
            hs.at[side, k], hr.at[side, k], {"lat": other[side]})

    def spread(n, peer):
        return [
            remote(wind, own.at[v, :, pl.ds(0, 3)], gs.at[n, 0], gr.at[n, 0], {"vec": peer}),
            remote(depth, own.at[v, :, 3], gs.at[n, 1], gr.at[n, 1], {"vec": peer}),
        ]

    def passed(side, n, peer):
        made = []
        for s in range(steps - 1):
            at = edge[side](reach - 1 - s)
            made.append(remote(
                ring.at[v, s, :, at, :], ring.at[v, s, :, at, :],
                fs.at[side, n, s], fr.at[side, n, s], {"vec": peer}))
        return made

    for side in range(2):
        @pl.when(has[side])
        def _(side=side):
            for copy in edges(side):
                copy.start()

    @pl.loop(0, count)
    def _(k):
        for side in range(2):
            @pl.when(has[side])
            def _(side=side):
                state(side, k).start()

    for n, peer in enumerate(peers):
        for copy in spread(n, peer):
            copy.start()

    for side in range(2):
        @pl.when(has[1 - side])
        def _(side=side):
            for copy in edges(side):
                copy.wait_recv()
            for n, peer in enumerate(peers):
                for copy in passed(side, n, peer):
                    copy.start()

    for copy in local:
        copy.wait()
    for n, peer in enumerate(peers):
        for copy in spread(n, peer):
            copy.wait_recv()
    for side in range(2):
        @pl.when(has[1 - side])
        def _(side=side):
            for n, peer in enumerate(peers):
                for copy in passed(side, n, peer):
                    copy.wait_recv()

    row = lax.broadcasted_iota(jnp.int32, (8, LANES), 0)

    @pl.loop(0, count)
    def _(k):
        for side in range(2):
            @pl.when(has[1 - side])
            def _(side=side):
                state(side, k).wait_recv()

        def span(t):
            return pl.ds(t * LANES, LANES)

        def first(side, f, t):
            return (x, halo)[side][k, f, :, span(t)]

        def reader(ref):
            return lambda side, f, t: ref[side, f, :, span(t)]

        def writer(ref):
            def put(side, f, t, value):
                ref[side, f, :, span(t)] = value
            return put

        def last(side, f, t, value):
            out[k, f, :, span(t)] = value

        for s in range(steps):
            def coefficient(side, channel, t, s=s):
                block, offset = divmod(t * LANES, part)
                return (own, ring)[side][block, s, channel, :, pl.ds(offset, LANES)]

            final = s == steps - 1
            good = reach - 1 - s
            keep = ((row < good) & has[1]) | ((row >= rows - good) & has[0])
            sweep(
                first if s == 0 else reader((ping, pong)[(s - 1) % 2]),
                last if final else writer((ping, pong)[s % 2]),
                coefficient, (0,) if final else (0, 1), tiles, keep)
        pltpu.make_async_copy(out.at[k], out_hbm.at[k], out_sem.at[k]).start()

    for side in range(2):
        @pl.when(has[side])
        def _(side=side):
            for copy in edges(side):
                copy.wait_send()
        @pl.when(has[1 - side])
        def _(side=side):
            for n, peer in enumerate(peers):
                for copy in passed(side, n, peer):
                    copy.wait_send()
    for n, peer in enumerate(peers):
        for copy in spread(n, peer):
            copy.wait_send()

    @pl.loop(0, count)
    def _(k):
        for side in range(2):
            @pl.when(has[side])
            def _(side=side):
                state(side, k).wait_send()
        pltpu.make_async_copy(out.at[k], out_hbm.at[k], out_sem.at[k]).wait()


def solution(mesh):
    nv, nl = mesh.shape["vec"], mesh.shape["lat"]

    def shards(perturbation, wind_coriolis, depth_field):
        count, _, rows, width = perturbation.shape
        steps, part = wind_coriolis.shape[0], wind_coriolis.shape[3]
        dma = pltpu.SemaphoreType.DMA
        f32 = jnp.float32
        return pl.pallas_call(
            functools.partial(kernel, nv, nl),
            out_shape=jax.ShapeDtypeStruct(perturbation.shape, f32),
            in_specs=[pl.BlockSpec(memory_space=pl.ANY)] * 3,
            out_specs=pl.BlockSpec(memory_space=pl.ANY),
            scratch_shapes=[
                pltpu.VMEM((count, 3, rows, width), f32),
                pltpu.VMEM((count, 3, rows, width), f32),
                pltpu.VMEM((2, 3, rows, width), f32),
                pltpu.VMEM((2, 3, rows, width), f32),
                pltpu.VMEM((count, 3, rows, width), f32),
                pltpu.VMEM((nv, steps, 4, rows, part), f32),
                pltpu.VMEM((nv, steps - 1, 4, rows, part), f32),
                dma((1,)), dma((2,)), dma((count,)),
                dma((nv - 1, 2)), dma((nv - 1, 2)),
                dma((2, steps - 1, 2)), dma((2, steps - 1, 2)),
                dma((2, nv - 1, steps - 1)), dma((2, nv - 1, steps - 1)),
                dma((2, count)), dma((2, count)),
            ],
            compiler_params=pltpu.CompilerParams(
                collective_id=0, has_side_effects=True, vmem_limit_bytes=40 * 1024 * 1024
            ),
        )(perturbation, wind_coriolis, depth_field)

    placed = (P("vec", None, "lat", None), P(None, None, "lat", "vec"), P(None, "lat", "vec"))
    return jax.shard_map(
        shards, mesh=mesh, in_specs=placed, out_specs=P("vec", None, "lat", None), check_vma=False
    )
```

time: 80.7 us -> 47.3 us (0.59)
  Pallas kernels: 0 us -> 42.8 us
  blocking collectives: 25.9 us -> 0 us
  starting transfers between devices: 24.7 us -> 0 us
  other arithmetic: 12.6 us -> 0 us
  waiting for transfers between devices: 9.72 us -> 0 us
  local copies, waits for them, and re-layouts: 7.08 us -> 4.32 us
    pallas_call x0 -> x1, Pallas kernels: none -> 42.8 us  [shards(): pl.pallas_call(functools.partial(kernel, nv, nl), out_shape=jax.ShapeDtyp...]
    all_gather x4 -> x0, blocking collectives: 25.9 us -> none  [shards(): gathered = lax.all_gather(coefficients[moment], 'vec', axis=2, tiled=True)]
    ppermute x8 -> x0, starting transfers between devices: 24.7 us -> none  [the longest x4 15.5 us: extended(): after = lax.ppermute(leading, axis, down)]
    ppermute x8 -> x0, waiting for transfers between devices: 9.72 us -> none  [the longest x4 7.17 us: extended(): after = lax.ppermute(leading, axis, down)]
    another operation x13 -> x0, other arithmetic: 8.52 us -> none  [advance(): return jnp.stack([new_height, new_zonal, new_north], axis=-3)]
    slice x23 -> x0, local copies, waits for them, and re-layouts: 5.71 us -> none  [the longest x22 3.37 us: lon_diff(): return 0.5 * (jnp.roll(field, -1, axis=-1) - jnp.roll(field, 1, axis=-1))]
    unnamed x2 -> x7, local copies, waits for them, and re-layouts: 0.01 us -> 4.32 us
    concatenate x5 -> x0, other arithmetic: 3.19 us -> none  [the longest x4 2.23 us: extended(): shard = jnp.concatenate([before, shard, after], axis=dim)]
  transfers between devices with their start and end apart: 8 -> 0, of which waited for: 4 -> 0; matrix products, arithmetic and copies ran while one was open for 1% -> 0% of each run, Pallas kernels for 0% -> 0%
where the time goes in v1:
time: 47.3 us; the launch traced here: 47.1 us
  Pallas kernels  42.8 us (90%)
  local copies, waits for them, and re-layouts  4.32 us (9%)
    pallas_call x1, Pallas kernels, shards(): pl.pallas_call(functools.partial(kernel, nv, nl), out_shape=jax.ShapeDtyp...  42.8 us
    unnamed x7, local copies, waits for them, and re-layouts  4.32 us

profile of v1, /device:TPU:9, one launch (start us, length us, event | category | flops | bytes accessed | tf_op | source)
XLA Modules:
  0.0 47.1 jit_solution(8240718816434718974)
XLA Ops:
  0.0 0.0 copy-start
  0.0 1.4 %copy-done = f32[8,3,8,2048]{3,2,1,0:T(8,128)S(1)} copy-done((f32[8,3,8,2048]{3,2,1,0:T(8,128)S(1)}, f32[8,3,8,2048]{3,2,1,0:T(8,128)}, u32[]{:S(2)}) %copy-start) | copy-done | bytes 1572888
  1.4 0.0 copy-start.1
  1.4 0.9 %copy-done.1 = f32[4,3,8,512]{3,2,1,0:T(8,128)S(1)} copy-done((f32[4,3,8,512]{3,2,1,0:T(8,128)S(1)}, f32[4,3,8,512]{3,2,1,0:T(8,128)}, u32[]{:S(2)}) %copy-start.1) | copy-done | bytes 196632
  2.3 0.0 copy-start.2
  2.3 0.8 %copy-done.2 = f32[4,8,512]{2,1,0:T(8,128)S(1)} copy-done((f32[4,8,512]{2,1,0:T(8,128)S(1)}, f32[4,8,512]{2,1,0:T(8,128)}, u32[]{:S(2)}) %copy-start.2) | copy-done | bytes 65560
  3.2 42.8 %shard_map.37 = f32[8,3,8,2048]{3,2,1,0:T(8,128)S(1)} custom-call(f32[8,3,8,2048]{3,2,1,0:T(8,128)S(1)} %copy-done, f32[4,3,8,512]{3,2,1,0:T(8,128)S(1)} %copy-done.1, f32[4,8,512]{2,1,0:T(8,128)S(1)} %copy-done.2), custom_call_target="tpu_custom_call" | custom-call | tf_op jit(solution)/shard_map/pallas_call | solution.py:251
  46.0 1.1 %copy.5 = f32[8,3,8,2048]{3,2,1,0:T(8,128)} copy(f32[8,3,8,2048]{3,2,1,0:T(8,128)S(1)} %shard_map.37) | data formatting | bytes 3145728
Async XLA Ops:
  0.0 1.4 %copy-start = (f32[8,3,8,2048]{3,2,1,0:T(8,128)S(1)}, f32[8,3,8,2048]{3,2,1,0:T(8,128)}, u32[]{:S(2)}) copy-start(f32[8,3,8,2048]{3,2,1,0:T(8,128)} %x_hbm.1) | copy-start | bytes 4718596
  1.4 0.9 %copy-start.1 = (f32[4,3,8,512]{3,2,1,0:T(8,128)S(1)}, f32[4,3,8,512]{3,2,1,0:T(8,128)}, u32[]{:S(2)}) copy-start(f32[4,3,8,512]{3,2,1,0:T(8,128)} %wind.1) | copy-start | bytes 589828
  2.3 0.8 %copy-start.2 = (f32[4,8,512]{2,1,0:T(8,128)S(1)}, f32[4,8,512]{2,1,0:T(8,128)}, u32[]{:S(2)}) copy-start(f32[4,8,512]{2,1,0:T(8,128)} %depth.1) | copy-start | bytes 196612

commit v2 on v1

--- a/solution.py
+++ b/solution.py
@@ -65,9 +65,9 @@
 
 def kernel(
     nv, nl, x_hbm, wind, depth, out_hbm,
-    x, halo, ping, pong, out, own, ring,
+    x, halo, transit, ping, pong, out, own, ring,
     x_sem, own_sem, out_sem,
-    gs, gr, cs, cr, fs, fr, hs, hr,
+    gs, gr, cs, cr, fs, fr, hs, hr, ts, tr,
 ):
     count, _, rows, width = x_hbm.shape
     steps, part = wind.shape[0], wind.shape[3]
@@ -75,6 +75,23 @@
     v, l = lax.axis_index("vec"), lax.axis_index("lat")
     has = (l > 0, l < nl - 1)
     other = (l - 1, l + 1)
+    far = (l - 2, l + 2)
+    reaches = (l > 1, l < nl - 2)
+    pairs = nl // 2
+    odd = lax.rem(l, 2)
+    place = l // 2
+
+    def share(number, wanted):
+        return jnp.where(wanted, number * count // pairs, 0) if nl % 2 == 0 else jnp.int32(0)
+
+    relayed = (
+        share(place, (odd == 0) & reaches[0]),
+        share(pairs - 1 - place, (odd == 1) & reaches[1]),
+    )
+    relaying = (
+        share(place, (odd == 1) & reaches[0]),
+        share(pairs - 1 - place, (odd == 0) & reaches[1]),
+    )
     peers = [lax.rem(v + k, nv) for k in range(1, nv)]
     edge = (lambda n: pl.ds(0, n), lambda n: pl.ds(rows - n, n))
 
@@ -98,7 +115,10 @@
         @pl.when(has[side])
         def _(side=side):
             pl.semaphore_signal(barrier, inc=1, device_id={"lat": other[side]}, device_id_type=MESH)
-    pl.semaphore_wait(barrier, nv - 1 + has[0].astype(jnp.int32) + has[1].astype(jnp.int32))
+        @pl.when(reaches[side])
+        def _(side=side):
+            pl.semaphore_signal(barrier, inc=1, device_id={"lat": far[side]}, device_id_type=MESH)
+    pl.semaphore_wait(barrier, nv - 1 + sum(flag.astype(jnp.int32) for flag in has + reaches))
 
     def remote(src, dst, send, recv, target):
         return pltpu.make_async_remote_copy(
@@ -124,6 +144,18 @@
             x_hbm.at[k, :, at, :], halo.at[k, :, at, :],
             hs.at[side, k], hr.at[side, k], {"lat": other[side]})
 
+    def detour(side, k):
+        at = edge[side](reach)
+        return remote(
+            x_hbm.at[k, :, at, :], transit.at[k, :, at, :],
+            hs.at[side, k], tr.at[k], {"lat": other[1 - side]})
+
+    def onward(side, k):
+        at = edge[side](reach)
+        return remote(
+            transit.at[k, :, at, :], halo.at[k, :, at, :],
+            ts.at[k], hr.at[side, k], {"lat": far[side]})
+
     def spread(n, peer):
         return [
             remote(wind, own.at[v, :, pl.ds(0, 3)], gs.at[n, 0], gr.at[n, 0], {"vec": peer}),
@@ -148,7 +180,14 @@
     @pl.loop(0, count)
     def _(k):
         for side in range(2):
-            @pl.when(has[side])
+            @pl.when(k < relayed[side])
+            def _(side=side):
+                detour(side, k).start()
+
+    @pl.loop(0, count)
+    def _(k):
+        for side in range(2):
+            @pl.when(has[side] & (k >= relayed[side]))
             def _(side=side):
                 state(side, k).start()
 
@@ -165,6 +204,13 @@
                 for copy in passed(side, n, peer):
                     copy.start()
 
+    @pl.loop(0, count)
+    def _(k):
+        for side in range(2):
+            @pl.when(k < relaying[side])
+            def _(side=side):
+                detour(side, k).wait_recv()
+                onward(side, k).start()
     for copy in local:
         copy.wait()
     for n, peer in enumerate(peers):
@@ -237,6 +283,9 @@
             @pl.when(has[side])
             def _(side=side):
                 state(side, k).wait_send()
+            @pl.when(k < relaying[side])
+            def _(side=side):
+                onward(side, k).wait_send()
         pltpu.make_async_copy(out.at[k], out_hbm.at[k], out_sem.at[k]).wait()
 
 
@@ -251,9 +300,10 @@
         return pl.pallas_call(
             functools.partial(kernel, nv, nl),
             out_shape=jax.ShapeDtypeStruct(perturbation.shape, f32),
-            in_specs=[pl.BlockSpec(memory_space=pl.ANY)] * 3,
+            in_specs=[pl.BlockSpec(memory_space=pltpu.HBM)] * 3,
             out_specs=pl.BlockSpec(memory_space=pl.ANY),
             scratch_shapes=[
+                pltpu.VMEM((count, 3, rows, width), f32),
                 pltpu.VMEM((count, 3, rows, width), f32),
                 pltpu.VMEM((count, 3, rows, width), f32),
                 pltpu.VMEM((2, 3, rows, width), f32),
@@ -265,12 +315,12 @@
                 dma((nv - 1, 2)), dma((nv - 1, 2)),
                 dma((2, steps - 1, 2)), dma((2, steps - 1, 2)),
                 dma((2, nv - 1, steps - 1)), dma((2, nv - 1, steps - 1)),
-                dma((2, count)), dma((2, count)),
+                dma((2, count)), dma((2, count)), dma((count,)), dma((count,)),
             ],
             compiler_params=pltpu.CompilerParams(
                 collective_id=0, has_side_effects=True, vmem_limit_bytes=40 * 1024 * 1024
             ),
-        )(perturbation, wind_coriolis, depth_field)
+        )(*(pltpu.with_memory_space_constraint(a, pltpu.HBM) for a in (perturbation, wind_coriolis, depth_field)))
 
     placed = (P("vec", None, "lat", None), P(None, None, "lat", "vec"), P(None, "lat", "vec"))
     return jax.shard_map(

time: 47.3 us -> 40.5 us (0.86)
  Pallas kernels: 42.8 us -> 38.8 us
  local copies, waits for them, and re-layouts: 4.32 us -> 1.15 us
    pallas_call x1, Pallas kernels: 42.8 us -> 38.8 us  [shards(): pl.pallas_call(functools.partial(kernel, nv, nl), out_shape=jax.ShapeDtyp...]
    unnamed x7 -> x1, local copies, waits for them, and re-layouts: 4.32 us -> 1.15 us
where the time goes in v2:
time: 40.5 us; the launch traced here: 40 us
  Pallas kernels  38.8 us (96%)
  local copies, waits for them, and re-layouts  1.15 us (3%)
    pallas_call x1, Pallas kernels, shards(): pl.pallas_call(functools.partial(kernel, nv, nl), out_shape=jax.ShapeDtyp...  38.8 us
    unnamed x1, local copies, waits for them, and re-layouts  1.15 us

profile of v2, /device:TPU:9, one launch (start us, length us, event | category | flops | bytes accessed | tf_op | source)
XLA Modules:
  0.0 40.0 jit_solution(15694873030479225161)
XLA Ops:
  0.0 38.8 %shard_map.37 = f32[8,3,8,2048]{3,2,1,0:T(8,128)S(1)} custom-call(f32[8,3,8,2048]{3,2,1,0:T(8,128)} %x_hbm.1, f32[4,3,8,512]{3,2,1,0:T(8,128)} %wind.1, f32[4,8,512]{2,1,0:T(8,128)} %depth.1), custom_call_target="tpu_custom_call" | custom-call | tf_op jit(solution)/shard_map/pallas_call | solution.py:300
  38.8 1.1 %copy.5 = f32[8,3,8,2048]{3,2,1,0:T(8,128)} copy(f32[8,3,8,2048]{3,2,1,0:T(8,128)S(1)} %shard_map.37) | data formatting | bytes 3145728

commit v3 on v2

--- a/solution.py
+++ b/solution.py
@@ -44,12 +44,7 @@
                 rise[side, field] = jnp.where(last_row, turned[1 - side][0], turned[side][0])
                 fall[side, field] = jnp.where(first_row, turned[1 - side][1], turned[side][1])
         for side in sides:
-            a = half_step * coefficient(side, 0, t)
-            b = half_step * coefficient(side, 1, t)
-            d = time_step * coefficient(side, 2, t)
-            c = half_step * coefficient(side, 3, t)
-            to_east, to_west = side_weight - a, side_weight + a
-            to_rise, to_fall = side_weight - b, side_weight + b
+            to_east, to_west, to_rise, to_fall, d, c = (coefficient(side, q, t) for q in range(6))
             new = [
                 (1.0 - 4.0 * side_weight) * here[side, f]
                 + (to_east * east[side, f] + to_west * west[side, f])
@@ -64,9 +59,9 @@
 
 
 def kernel(
-    nv, nl, x_hbm, wind, depth, out_hbm,
-    x, halo, transit, ping, pong, out, own, ring,
-    x_sem, own_sem, out_sem,
+    nv, nl, x_hbm, wind, depth, out,
+    x, halo, transit, ping, pong, own, ring, table,
+    x_sem, own_sem,
     gs, gr, cs, cr, fs, fr, hs, hr, ts, tr,
 ):
     count, _, rows, width = x_hbm.shape
@@ -103,11 +98,6 @@
     for copy in local:
         copy.start()
 
-    for side in range(2):
-        @pl.when(jnp.logical_not(has[1 - side]))
-        def _(side=side):
-            halo[:, :, edge[side](reach), :] = jnp.zeros((count, 3, reach, width), jnp.float32)
-
     barrier = pltpu.get_barrier_semaphore()
     for peer in peers:
         pl.semaphore_signal(barrier, inc=1, device_id={"vec": peer}, device_id_type=MESH)
@@ -196,6 +186,11 @@
             copy.start()
 
     for side in range(2):
+        @pl.when(jnp.logical_not(has[1 - side]))
+        def _(side=side):
+            halo[:, :, edge[side](reach), :] = jnp.zeros((count, 3, reach, width), jnp.float32)
+
+    for side in range(2):
         @pl.when(has[1 - side])
         def _(side=side):
             for copy in edges(side):
@@ -223,6 +218,18 @@
                 for copy in passed(side, n, peer):
                     copy.wait_recv()
 
+    for side in range(2):
+        @pl.loop(0, steps - side)
+        def _(s, side=side):
+            for t in range(tiles):
+                block, offset = divmod(t * LANES, part)
+                given = (own, ring)[side]
+                a, b, d, c = (given[block, s, q, :, pl.ds(offset, LANES)] for q in range(4))
+                a, b = half_step * a, half_step * b
+                values = (side_weight - a, side_weight + a, side_weight - b, side_weight + b, time_step * d, half_step * c)
+                for q, value in enumerate(values):
+                    table[side, s, q, :, pl.ds(t * LANES, LANES)] = value
+
     row = lax.broadcasted_iota(jnp.int32, (8, LANES), 0)
 
     @pl.loop(0, count)
@@ -251,8 +258,7 @@
 
         for s in range(steps):
             def coefficient(side, channel, t, s=s):
-                block, offset = divmod(t * LANES, part)
-                return (own, ring)[side][block, s, channel, :, pl.ds(offset, LANES)]
+                return table[side, s, channel, :, span(t)]
 
             final = s == steps - 1
             good = reach - 1 - s
@@ -261,7 +267,6 @@
                 first if s == 0 else reader((ping, pong)[(s - 1) % 2]),
                 last if final else writer((ping, pong)[s % 2]),
                 coefficient, (0,) if final else (0, 1), tiles, keep)
-        pltpu.make_async_copy(out.at[k], out_hbm.at[k], out_sem.at[k]).start()
 
     for side in range(2):
         @pl.when(has[side])
@@ -286,7 +291,6 @@
             @pl.when(k < relaying[side])
             def _(side=side):
                 onward(side, k).wait_send()
-        pltpu.make_async_copy(out.at[k], out_hbm.at[k], out_sem.at[k]).wait()
 
 
 def solution(mesh):
@@ -301,17 +305,17 @@
             functools.partial(kernel, nv, nl),
             out_shape=jax.ShapeDtypeStruct(perturbation.shape, f32),
             in_specs=[pl.BlockSpec(memory_space=pltpu.HBM)] * 3,
-            out_specs=pl.BlockSpec(memory_space=pl.ANY),
+            out_specs=pl.BlockSpec(memory_space=pltpu.VMEM),
             scratch_shapes=[
                 pltpu.VMEM((count, 3, rows, width), f32),
                 pltpu.VMEM((count, 3, rows, width), f32),
                 pltpu.VMEM((count, 3, rows, width), f32),
                 pltpu.VMEM((2, 3, rows, width), f32),
                 pltpu.VMEM((2, 3, rows, width), f32),
-                pltpu.VMEM((count, 3, rows, width), f32),
                 pltpu.VMEM((nv, steps, 4, rows, part), f32),
                 pltpu.VMEM((nv, steps - 1, 4, rows, part), f32),
-                dma((1,)), dma((2,)), dma((count,)),
+                pltpu.VMEM((2, steps, 6, rows, width), f32),
+                dma((1,)), dma((2,)),
                 dma((nv - 1, 2)), dma((nv - 1, 2)),
                 dma((2, steps - 1, 2)), dma((2, steps - 1, 2)),
                 dma((2, nv - 1, steps - 1)), dma((2, nv - 1, steps - 1)),

time: 40.5 us -> 40 us (0.988)
    pallas_call x1, Pallas kernels: 38.8 us -> 38.4 us  [shards(): pl.pallas_call(functools.partial(kernel, nv, nl), out_shape=jax.ShapeDtyp...]
where the time goes in v3:
time: 40 us; the launch traced here: 39.5 us
  Pallas kernels  38.4 us (96%)
  local copies, waits for them, and re-layouts  1.15 us (3%)
    pallas_call x1, Pallas kernels, shards(): pl.pallas_call(functools.partial(kernel, nv, nl), out_shape=jax.ShapeDtyp...  38.4 us
    unnamed x1, local copies, waits for them, and re-layouts  1.15 us

profile of v3, /device:TPU:9, one launch (start us, length us, event | category | flops | bytes accessed | tf_op | source)
XLA Modules:
  0.0 39.5 jit_solution(15222114259940555551)
XLA Ops:
  0.0 38.4 %shard_map.37 = f32[8,3,8,2048]{3,2,1,0:T(8,128)S(1)} custom-call(f32[8,3,8,2048]{3,2,1,0:T(8,128)} %x_hbm.1, f32[4,3,8,512]{3,2,1,0:T(8,128)} %wind.1, f32[4,8,512]{2,1,0:T(8,128)} %depth.1), custom_call_target="tpu_custom_call" | custom-call | tf_op jit(solution)/shard_map/pallas_call | solution.py:304
  38.4 1.1 %copy.5 = f32[8,3,8,2048]{3,2,1,0:T(8,128)} copy(f32[8,3,8,2048]{3,2,1,0:T(8,128)S(1)} %shard_map.37) | data formatting | bytes 3145728

commit v4 on v3

--- a/solution.py
+++ b/solution.py
@@ -161,29 +161,33 @@
                 fs.at[side, n, s], fr.at[side, n, s], {"vec": peer}))
         return made
 
-    for side in range(2):
-        @pl.when(has[side])
-        def _(side=side):
-            for copy in edges(side):
-                copy.start()
-
-    @pl.loop(0, count)
-    def _(k):
-        for side in range(2):
-            @pl.when(k < relayed[side])
-            def _(side=side):
-                detour(side, k).start()
-
-    @pl.loop(0, count)
-    def _(k):
-        for side in range(2):
-            @pl.when(has[side] & (k >= relayed[side]))
-            def _(side=side):
-                state(side, k).start()
-
     for n, peer in enumerate(peers):
         for copy in spread(n, peer):
             copy.start()
+
+    for side in range(2):
+        @pl.when(has[side])
+        def _(side=side):
+            for copy in edges(side):
+                copy.start()
+
+    @pl.loop(0, count)
+    def _(k):
+        for side in range(2):
+            @pl.when(k < relayed[side])
+            def _(side=side):
+                detour(side, k).start()
+            @pl.when(has[side] & (odd == side) & (k >= relayed[side]))
+            def _(side=side):
+                state(side, k).start()
+
+    @pl.loop(0, count)
+    def _(k):
+        for side in range(2):
+            @pl.when(has[side] & (odd != side))
+            def _(side=side):
+                state(side, k).start()
+
 
     for side in range(2):
         @pl.when(jnp.logical_not(has[1 - side]))

time: 40 us -> 40 us (level)
  no operation moved by 1% of the time
where the time goes in v4:
time: 40 us; the launch traced here: 39.6 us
  Pallas kernels  38.4 us (96%)
  local copies, waits for them, and re-layouts  1.15 us (3%)
    pallas_call x1, Pallas kernels, shards(): pl.pallas_call(functools.partial(kernel, nv, nl), out_shape=jax.ShapeDtyp...  38.4 us
    unnamed x1, local copies, waits for them, and re-layouts  1.15 us

profile of v4, /device:TPU:9, one launch (start us, length us, event | category | flops | bytes accessed | tf_op | source)
XLA Modules:
  0.0 39.6 jit_solution(6740904035122738550)
XLA Ops:
  0.0 38.4 %shard_map.37 = f32[8,3,8,2048]{3,2,1,0:T(8,128)S(1)} custom-call(f32[8,3,8,2048]{3,2,1,0:T(8,128)} %x_hbm.1, f32[4,3,8,512]{3,2,1,0:T(8,128)} %wind.1, f32[4,8,512]{2,1,0:T(8,128)} %depth.1), custom_call_target="tpu_custom_call" | custom-call | tf_op jit(solution)/shard_map/pallas_call | solution.py:308
  38.4 1.1 %copy.5 = f32[8,3,8,2048]{3,2,1,0:T(8,128)} copy(f32[8,3,8,2048]{3,2,1,0:T(8,128)S(1)} %shard_map.37) | data formatting | bytes 3145728
